TPU v7x, 32 devices: a whole 2x2x4 slice. The times are simulated.
32 devices in a mesh: dp: 2 (over y), expert: 16 (over z, x, core).
Axes of the slice: x: 2, y: 2, z: 4, core: 2. Of those that a mesh axis runs over, the one named last changes fastest.
Arguments:
- tokens: bfloat16 [512, 2880], P(('dp', 'expert')), may hold values from -6 to 6
- grad_out: bfloat16 [512, 2880], P(('dp', 'expert')), may hold values from -6 to 6
- route_ids: int32 [512, 4], P(('dp', 'expert')), may hold values from 0 to 4, all different within a row; in each aligned block of 16 rows (0 to 15, 16 to 31, ...) at most 16 rows name the same one
- route_prob: float32 [512, 4], P(('dp', 'expert')), may hold values from 0.05 to 1
- device_expert: int32 [16], replicated, may hold values from 0 to 4, as said below
- unit_count: int32 [16], replicated, may hold values from 264 to 480, as said below
- expert_weights: bfloat16 [16, 480, 8640], P('expert'), may hold values from -0.109375 to 0.109375
Outputs:
- grad_tokens: bfloat16 [512, 2880], P(('dp', 'expert'))
- grad_weights: bfloat16 [16, 480, 8640], P('expert', 'dp')
Inputs may be any that keep to these rules, and one draw needn't show every extreme that they name: `route_ids`: each row names 4 different experts; the 16 rows of one device name each expert at most 16 times, and in every draw some device names some expert exactly 16 times. `device_expert`: aligned blocks of 16 indices of expert hold 5 experts, ids rising by one from 5 times the block's number; the indices of one expert are consecutive, 3 or 4 of them; every expert has a group. `unit_count`: the counts of the indices of one expert sum to 1440; rows of expert_weights at or past a slot's count are not part of the model.
All inputs are finite; a program needn't handle non-finite values.
Results may differ from a plain program's by a relative error of at most 0.0058.
Values may be sent and summed in bfloat16 or wider, within the bound.
A program may use at most 128 MiB of HBM per device.

v0:
```python
import jax
import jax.numpy as jnp
from jax import lax
from jax.sharding import PartitionSpec as P

AXES = ("dp", "expert")


def silu_parts(preact):
    sigma = jax.nn.sigmoid(preact)
    return (preact * sigma, sigma * (1.0 + preact * (1.0 - sigma)))


def unit_work(token_rows, grad_rows, slot_weights, unit_mask):
    width = token_rows.shape[1]
    gate_rows = slot_weights[:, :width]
    up_rows = slot_weights[:, width : 2 * width]
    down_rows = slot_weights[:, 2 * width :]
    contract = (((1,), (1,)), ((), ()))
    gate_pre = lax.dot_general(token_rows, gate_rows, contract, preferred_element_type=jnp.float32)
    up_pre = lax.dot_general(token_rows, up_rows, contract, preferred_element_type=jnp.float32)
    back_grad = lax.dot_general(grad_rows, down_rows, contract, preferred_element_type=jnp.float32)
    active, slope = silu_parts(gate_pre)
    hidden = (active * up_pre * unit_mask).astype(jnp.bfloat16)
    grad_gate = (back_grad * up_pre * slope * unit_mask).astype(jnp.bfloat16)
    grad_up = (back_grad * active * unit_mask).astype(jnp.bfloat16)
    partial_value = jnp.dot(grad_gate, gate_rows, preferred_element_type=jnp.float32) + jnp.dot(
        grad_up, up_rows, preferred_element_type=jnp.float32
    )
    return (partial_value, hidden, grad_gate, grad_up)


def weight_terms(token_rows, grad_rows, hidden, grad_gate, grad_up):
    rows_first = (((0,), (0,)), ((), ()))
    return jnp.concatenate(
        [
            lax.dot_general(grad_gate, token_rows, rows_first, preferred_element_type=jnp.float32),
            lax.dot_general(grad_up, token_rows, rows_first, preferred_element_type=jnp.float32),
            lax.dot_general(hidden, grad_rows, rows_first, preferred_element_type=jnp.float32),
        ],
        axis=1,
    )


def send_back(partial_value):
    return lax.all_to_all(partial_value, "expert", split_axis=0, concat_axis=0, tiled=True)


def routed_shards(
    tokens, grad_out, route_ids, route_prob, device_expert, unit_count, expert_weights
):
    token_count, width = tokens.shape
    top_count = route_ids.shape[1]
    devices = lax.axis_size("expert")
    experts = 5 * devices // 16
    capacity = token_count * top_count * 4 // devices
    flat_ids = route_ids.reshape(-1)
    onehot = (flat_ids[:, None] == jnp.arange(experts, dtype=jnp.int32)[None, :]).astype(jnp.int32)
    rank_of = jnp.sum(onehot * jnp.cumsum(onehot, axis=0), axis=1) - 1
    picked = (flat_ids[None, None, :] == device_expert[:, None, None]) & (
        rank_of[None, None, :] == jnp.arange(capacity, dtype=jnp.int32)[None, :, None]
    )
    picked = picked.astype(jnp.float32).reshape(devices * capacity, token_count * top_count)
    by_token = picked.reshape(devices * capacity, token_count, top_count).sum(axis=2)
    route_scale = jnp.dot(picked, route_prob.reshape(-1), precision=lax.Precision.HIGHEST)
    by_token_low = by_token.astype(jnp.bfloat16)
    sent_rows = jnp.dot(by_token_low, tokens, preferred_element_type=jnp.float32).astype(
        jnp.bfloat16
    )
    sent_grads = (
        route_scale[:, None] * jnp.dot(by_token_low, grad_out, preferred_element_type=jnp.float32)
    ).astype(jnp.bfloat16)
    outgoing = jnp.stack([sent_rows, sent_grads], axis=1).reshape(devices, capacity, 2, width)
    position = lax.axis_index("expert")
    unit_limit = lax.dynamic_index_in_dim(unit_count, position, keepdims=False)
    slot_weights = expert_weights[0]
    slot_units = slot_weights.shape[0]
    unit_mask = (jnp.arange(slot_units, dtype=jnp.int32) < unit_limit).astype(jnp.float32)
    arrived = lax.all_to_all(outgoing, "expert", split_axis=0, concat_axis=0, tiled=True)
    row_pairs = arrived.reshape(-1, 2, width)
    partial_value, hidden, grad_gate, grad_up = unit_work(
        row_pairs[:, 0], row_pairs[:, 1], slot_weights, unit_mask
    )
    leading = (arrived.shape[0], arrived.shape[1])
    returned, all_rows, hidden, grad_gate, grad_up = (
        send_back(partial_value.reshape(leading + (width,))),
        arrived,
        hidden.reshape(leading + (slot_units,)),
        grad_gate.reshape(leading + (slot_units,)),
        grad_up.reshape(leading + (slot_units,)),
    )
    row_pairs = all_rows.reshape(-1, 2, width)
    token_rows = row_pairs[:, 0]
    grad_rows = row_pairs[:, 1]
    hidden = hidden.reshape(-1, slot_units)
    grad_gate = grad_gate.reshape(-1, slot_units)
    grad_up = grad_up.reshape(-1, slot_units)
    term_block = weight_terms(token_rows, grad_rows, hidden, grad_gate, grad_up)
    grad_weights = lax.psum_scatter(term_block, "dp", scatter_dimension=0, tiled=True)
    parts = returned.reshape(devices * capacity, width)
    grad_tokens = lax.dot_general(
        by_token,
        parts,
        (((0,), (0,)), ((), ())),
        precision=lax.Precision.HIGHEST,
        preferred_element_type=jnp.float32,
    )
    return (grad_tokens.astype(jnp.bfloat16), grad_weights.astype(jnp.bfloat16)[None])


def dense_shards(
    tokens, grad_out, route_ids, route_prob, device_expert, unit_count, expert_weights
):
    width = tokens.shape[1]
    devices = lax.axis_size("expert")
    experts = 5 * devices // 16
    half = expert_weights.shape[1] // lax.axis_size("dp")
    named = route_ids[:, :, None] == jnp.arange(experts, dtype=jnp.int32)[None, None, :]
    scales = jnp.sum(jnp.where(named, route_prob[:, :, None], 0.0), axis=1)
    x = lax.all_gather(tokens, AXES, axis=0, tiled=True)
    grads = lax.all_gather(grad_out, AXES, axis=0, tiled=True)
    scales = lax.all_gather(scales, AXES, axis=0, tiled=True)
    position = lax.axis_index("expert")
    expert = lax.dynamic_index_in_dim(device_expert, position, keepdims=False)
    limit = lax.dynamic_index_in_dim(unit_count, position, keepdims=False)
    scale = jnp.sum(jnp.where(jnp.arange(experts)[None, :] == expert, scales, 0.0), axis=1)
    dy = (scale[:, None] * grads.astype(jnp.float32)).astype(jnp.bfloat16)
    first = lax.axis_index("dp") * half
    weights = lax.dynamic_slice_in_dim(expert_weights[0], first, half, axis=0)
    mask = (first + jnp.arange(half, dtype=jnp.int32) < limit)[None, :]
    gate, up, down = (weights[:, i * width : (i + 1) * width] for i in range(3))
    contract = (((1,), (1,)), ((), ()))
    rows_first = (((0,), (0,)), ((), ()))
    f32 = jnp.float32
    g = lax.dot_general(x, gate, contract, preferred_element_type=f32)
    v = lax.dot_general(x, up, contract, preferred_element_type=f32)
    b = lax.dot_general(dy, down, contract, preferred_element_type=f32)
    sigma = jax.nn.sigmoid(g)
    active = g * sigma
    slope = sigma * (1.0 + g * (1.0 - sigma))
    hidden = jnp.where(mask, active * v, 0.0).astype(jnp.bfloat16)
    grad_gate = jnp.where(mask, b * v * slope, 0.0).astype(jnp.bfloat16)
    grad_up = jnp.where(mask, b * active, 0.0).astype(jnp.bfloat16)
    partial = jnp.dot(grad_gate, gate, preferred_element_type=f32) + jnp.dot(
        grad_up, up, preferred_element_type=f32
    )
    grad_tokens = lax.psum_scatter(partial, AXES, scatter_dimension=0, tiled=True)
    grad_weights = jnp.concatenate(
        [
            lax.dot_general(a, c, rows_first, preferred_element_type=f32).astype(jnp.bfloat16)
            for a, c in ((grad_gate, x), (grad_up, x), (hidden, dy))
        ],
        axis=1,
    )
    return (grad_tokens.astype(jnp.bfloat16), grad_weights[None])


def shards(tokens, grad_out, route_ids, *rest):
    token_count = tokens.shape[0]
    capacity = token_count * route_ids.shape[1] * 4 // lax.axis_size("expert")
    form = dense_shards if capacity >= token_count else routed_shards
    return form(tokens, grad_out, route_ids, *rest)


def solution(mesh):
    in_specs = (P(AXES, None),) * 4 + (P(), P(), P("expert", None, None))
    out_specs = (P(AXES, None), P("expert", "dp", None))
    return jax.shard_map(shards, mesh=mesh, in_specs=in_specs, out_specs=out_specs, check_vma=False)
```

profile of v0, /device:TPU:0, one launch (start us, length us, event | category | flops | bytes accessed | tf_op | source)
XLA Modules:
  0.0 294.3 jit_solution(11033249698941787515)
XLA Ops:
  7.2 0.0 all-gather.6.cloned.1.call-start
  7.2 0.7 all-gather.6.cloned.1.call-update
  7.9 0.0 all-gather.4.cloned.1.call-start
  7.9 0.7 all-gather.4.cloned.1.call-update
  8.6 0.0 reduce-scatter.2.cloned.1.call-start
  8.7 1.2 dynamic_slice.12
  9.9 1.2 dynamic_slice.13
  11.2 0.7 select_reduce_fusion.1
  11.9 43.8 %all-gather = f32[32,16,5]{1,2,0:T(8,128)S(1)} all-gather(f32[1,16,5]{1,2,0:T(8,128)S(1)} %bitcast.21), channel_id=1, replica_groups=mesh['dp'=2,'expert'=16] {'dp','expert'}, dimensions={0}, use_global_device_ids=true | all-gather | bytes 10560 | tf_op jit(solution)/shard_map/all_gather | solution.py:122
  55.7 0.1 reshape.19
  55.8 0.7 add_compare_fusion
  56.5 0.7 iota_compare_fusion.1
  57.1 0.1 select_reduce_fusion
  57.2 4.5 %dynamic-slice_bitcast_fusion = bf16[240,8640]{1,0:T(8,128)(2,1)} fusion(bf16[1,480,8640]{2,1,0:T(8,128)(2,1)} %param.13, s32[]{:T(128)S(6)} %select_n.29), kind=kLoop, calls=%fused_computation.2 | loop fusion | bytes 8294404 | tf_op jit(solution)/shard_map/dynamic_slice | solution.py:129
  61.7 10.9 %all-gather.6.cloned.1.call-done = bf16[512,2880]{1,0:T(8,128)(2,1)} async-done(((bf16[16,2880]{1,0:T(8,128)(2,1)}), bf16[512,2880]{1,0:T(8,128)(2,1)}) %all-gather.6.cloned.1.call-update) | async-done | bytes 2949136 | tf_op jit(solution)/shard_map/all_gather | solution.py:120
  72.6 4.2 %fusion.12 = f32[512,240]{0,1:T(8,128)} fusion(bf16[512,2880]{1,0:T(8,128)(2,1)} %all-gather.6.cloned.1.call-done, bf16[240,8640]{1,0:T(8,128)(2,1)} %dynamic-slice_bitcast_fusion), kind=kOutput, calls=%fused_computation.16 | convolution fusion | flops 707788800 | bytes 4919296 | tf_op jit(solution)/shard_map/dot_general | solution.py:135
  76.8 0.0 copy-done
  76.8 3.2 %fusion.9 = f32[512,240]{0,1:T(8,128)} fusion(bf16[512,2880]{1,0:T(8,128)(2,1)S(1)} %copy-done, bf16[240,8640]{1,0:T(8,128)(2,1)} %dynamic-slice_bitcast_fusion), kind=kOutput, calls=%fused_computation.15 | convolution fusion | flops 707788800 | bytes 4853760 | tf_op jit(solution)/shard_map/dot_general | solution.py:136
  80.0 53.1 %all-gather.4.cloned.1.call-done = bf16[512,2880]{1,0:T(8,128)(2,1)} async-done(((bf16[16,2880]{1,0:T(8,128)(2,1)}), bf16[512,2880]{1,0:T(8,128)(2,1)}) %all-gather.4.cloned.1.call-update) | async-done | bytes 2949136 | tf_op jit(solution)/shard_map/all_gather | solution.py:121
  133.1 3.9 %select_convert_fusion.1 = (bf16[512,240]{0,1:T(8,128)(2,1)S(1)}, bf16[512,240]{0,1:T(8,128)(2,1)S(1)}) fusion(pred[240]{0:T(512)(128)(4,1)S(1)} %add_compare_fusion, f32[512,240]{0,1:T(8,128)} %fusion.12, f32[512,240]{0,1:T(8,128)} %fusion.9, bf16[240,8640]{1,0:T(8,128)(2,1)} %dynamic-slice_bitcast_fusion, ...), kind=kOutput, calls=%fused_computation.18 | convolution fusion | flops 714055680 | bytes 5904624 | tf_op jit(solution)/shard_map/dot_general | solution.py:137
  137.0 0.0 copy-done.1
  137.0 1.0 fusion.2
  138.0 3.7 %convolution_add_fusion = f32[512,2880]{1,0:T(8,128)} fusion(f32[512,2880]{1,0:T(8,128)S(1)} %fusion.2, bf16[512,240]{0,1:T(8,128)(2,1)S(1)} %get-tuple-element.2, bf16[240,8640]{1,0:T(8,128)(2,1)S(1)} %copy-done.1), kind=kOutput, calls=%fused_computation.1 | convolution fusion | flops 709263360 | bytes 13586432 | tf_op jit(solution)/shard_map/dot_general | solution.py:144
  141.8 0.0 reduce-scatter.2.cloned.1.call-update
  141.8 2.0 convolution_convert_fusion.1
  143.8 2.0 convolution_convert_fusion.2
  145.9 0.1 copy-done.5
  146.0 0.4 copy-done.6
  146.4 2.3 convolution_convert_fusion
  148.7 7.5 %concatenate.3 = bf16[240,8640]{1,0:T(8,128)(2,1)} concatenate(bf16[240,2880]{1,0:T(8,128)(2,1)S(1)} %copy-done.3, bf16[240,2880]{1,0:T(8,128)(2,1)S(1)} %copy-done.2, bf16[240,2880]{1,0:T(8,128)(2,1)} %convolution_convert_fusion), dimensions={1} | concatenate | bytes 8294400 | tf_op jit(solution)/shard_map/concatenate | solution.py:148
  156.2 130.0 %reduce-scatter.2.cloned.1.call-done = f32[16,2880]{1,0:T(8,128)} async-done(((f32[512,2880]{1,0:T(8,128)}), f32[16,2880]{1,0:T(8,128)}) %reduce-scatter.2.cloned.1.call-update) | async-done | bytes 184336 | tf_op jit(solution)/shard_map/reduce_scatter | solution.py:147
  286.2 1.6 convert_element_type.31
  (11 shorter events, 0.0 us)
Async XLA Ops:
  7.2 65.4 %all-gather.6.cloned.1.call-start = ((), (), s32[]{:S(2)}) async-start(), calls=%async_computation.2 | async-start | bytes 3108864 | tf_op jit(solution)/shard_map/all_gather | solution.py:120
  7.9 125.2 %all-gather.4.cloned.1.call-start = ((), (), s32[]{:S(2)}) async-start(), calls=%async_computation.1 | async-start | bytes 3108864 | tf_op jit(solution)/shard_map/all_gather | solution.py:121
  8.6 277.5 %reduce-scatter.2.cloned.1.call-start = ((), (), s32[]{:S(2)}) async-start(), calls=%async_computation.3 | async-start | bytes 6217728 | tf_op jit(solution)/shard_map/reduce_scatter | solution.py:147
  72.6 4.2 %copy-start = (bf16[512,2880]{1,0:T(8,128)(2,1)S(1)}, bf16[512,2880]{1,0:T(8,128)(2,1)}, u32[]{:S(2)}) copy-start(bf16[512,2880]{1,0:T(8,128)(2,1)} %all-gather.6.cloned.1.call-done) | copy-start | bytes 8847364
  133.1 3.9 %copy-start.1 = (bf16[240,8640]{1,0:T(8,128)(2,1)S(1)}, bf16[240,8640]{1,0:T(8,128)(2,1)}, u32[]{:S(2)}) copy-start(bf16[240,8640]{1,0:T(8,128)(2,1)} %dynamic-slice_bitcast_fusion) | copy-start | bytes 12441604
  143.8 2.0 copy-start.4
  143.8 2.2 copy-start.5
  143.8 2.6 copy-start.6
  146.4 2.3 copy-start.2
  146.4 2.3 copy-start.3
Sparse Core Ops, SparseCore 0:
  10.8 61.7 all-gather.5
  75.4 57.5 all-gather.3
  141.9 144.2 reduce-scatter.1
where the time goes:
time: 295 us; the launch traced here: 294 us
  waiting for transfers between devices  195 us (66%)
  blocking collectives  43.8 us (15%)
  matrix products  22.4 us (8%)
  local copies, waits for them, and re-layouts  15.1 us (5%)
  between operations  13.8 us (5%)
  other arithmetic  3.68 us (1%)
    reduce_scatter x1, waiting for transfers between devices, dense_shards(): lax.psum_scatter(partial, AXES, scatter_dimension=0, tiled=True)  130 us
    all_gather x1, waiting for transfers between devices, dense_shards(): grads = lax.all_gather(grad_out, AXES, axis=0, tiled=True)  53.1 us
    all_gather x1, blocking collectives, dense_shards(): scales = lax.all_gather(scales, AXES, axis=0, tiled=True)  43.8 us
    all_gather x1, waiting for transfers between devices, dense_shards(): x = lax.all_gather(tokens, AXES, axis=0, tiled=True)  10.9 us
    concatenate x1, local copies, waits for them, and re-layouts, dense_shards(): jnp.concatenate([lax.dot_general(a, c, rows_first, preferred_element_type...  7.5 us
    dot_general x3, matrix products, dense_shards(): lax.dot_general(a, c, rows_first, preferred_element_type=f32)  6.33 us
  transfers between devices with their start and end apart: 3, of which 3 were waited for; matrix products, arithmetic and copies ran while one was open for 10% of the time, Pallas kernels for 0%

commit v1 on v0

--- a/solution.py
+++ b/solution.py
@@ -118,8 +118,11 @@
     named = route_ids[:, :, None] == jnp.arange(experts, dtype=jnp.int32)[None, None, :]
     scales = jnp.sum(jnp.where(named, route_prob[:, :, None], 0.0), axis=1)
     x = lax.all_gather(tokens, AXES, axis=0, tiled=True)
-    grads = lax.all_gather(grad_out, AXES, axis=0, tiled=True)
-    scales = lax.all_gather(scales, AXES, axis=0, tiled=True)
+    grads, scales = jnp.split(
+        lax.all_gather(jnp.concatenate([grad_out, scales], axis=1), AXES, axis=0, tiled=True),
+        [grad_out.shape[1]],
+        axis=1,
+    )
     position = lax.axis_index("expert")
     expert = lax.dynamic_index_in_dim(device_expert, position, keepdims=False)
     limit = lax.dynamic_index_in_dim(unit_count, position, keepdims=False)

time: 295 us -> 306 us (1.037)
  waiting for transfers between devices: 195 us -> 245 us
  blocking collectives: 43.8 us -> 0 us
  matrix products: 22.4 us -> 26.1 us
    all_gather x1 -> x0, blocking collectives: 43.8 us -> none  [dense_shards(): scales = lax.all_gather(scales, AXES, axis=0, tiled=True)]
    all_gather x1, waiting for transfers between devices: 10.9 us -> 53.6 us  [dense_shards(): x = lax.all_gather(tokens, AXES, axis=0, tiled=True)]
    all_gather x1, waiting for transfers between devices: 53.1 us -> 62.5 us  [dense_shards(): lax.all_gather(jnp.concatenate([grad_out, scales], axis=1), AXES, axis=0,...]
  transfers between devices with their start and end apart: 3 -> 3, of which waited for: 3 -> 3; matrix products, arithmetic and copies ran while one was open for 10% -> 11% of each run, Pallas kernels for 0% -> 0%
where the time goes in v1:
time: 306 us
  waiting for transfers between devices  245 us (80%)
  matrix products  26.1 us (9%)
  local copies, waits for them, and re-layouts  14.6 us (5%)
  between operations  13.8 us (5%)
  other arithmetic  6.44 us (2%)
    reduce_scatter x1, waiting for transfers between devices, dense_shards(): lax.psum_scatter(partial, AXES, scatter_dimension=0, tiled=True)  128 us
    all_gather x1, waiting for transfers between devices, dense_shards(): lax.all_gather(jnp.concatenate([grad_out, scales], axis=1), AXES, axis=0,...  62.5 us
    all_gather x1, waiting for transfers between devices, dense_shards(): x = lax.all_gather(tokens, AXES, axis=0, tiled=True)  53.6 us
    dot_general x3, matrix products, dense_shards(): lax.dot_general(a, c, rows_first, preferred_element_type=f32)  9.17 us
    concatenate x1, local copies, waits for them, and re-layouts, dense_shards(): jnp.concatenate([lax.dot_general(a, c, rows_first, preferred_element_type...  7.51 us
  transfers between devices with their start and end apart: 3, of which 3 were waited for; matrix products, arithmetic and copies ran while one was open for 11% of the time, Pallas kernels for 0%

profile of v1, /device:TPU:0, one launch (start us, length us, event | category | flops | bytes accessed | tf_op | source)
XLA Modules:
  0.0 305.6 jit_solution(10509964488103100096)
XLA Ops:
  7.2 0.0 all-gather.5.cloned.1.call-start
  7.2 0.7 all-gather.5.cloned.1.call-update
  7.9 0.0 all-gather.3.cloned.1.call-start
  7.9 0.7 select_reduce_fusion
  8.7 0.1 copy.11
  8.7 0.9 convert_element_type.27
  9.7 0.8 pad_maximum_fusion
  10.4 0.0 all-gather.3.cloned.1.call-update
  10.4 0.0 reduce-scatter.2.cloned.1.call-start
  10.5 1.2 dynamic_slice.12
  11.7 1.2 dynamic_slice.13
  13.0 0.7 add_compare_fusion
  13.6 0.7 iota_compare_fusion.1
  14.3 4.5 %dynamic-slice_bitcast_fusion = bf16[240,8640]{1,0:T(8,128)(2,1)} fusion(bf16[1,480,8640]{2,1,0:T(8,128)(2,1)} %param.13, s32[]{:T(128)S(6)} %select_n.29), kind=kLoop, calls=%fused_computation.3 | loop fusion | bytes 8294404 | tf_op jit(solution)/shard_map/dynamic_slice | solution.py:132
  18.8 53.6 %all-gather.5.cloned.1.call-done = bf16[512,2880]{1,0:T(8,128)(2,1)} async-done(((bf16[16,2880]{1,0:T(8,128)(2,1)}), bf16[512,2880]{1,0:T(8,128)(2,1)}) %all-gather.5.cloned.1.call-update) | async-done | bytes 2949136 | tf_op jit(solution)/shard_map/all_gather | solution.py:120
  72.4 4.2 %fusion.13 = f32[512,240]{0,1:T(8,128)} fusion(bf16[512,2880]{1,0:T(8,128)(2,1)} %all-gather.5.cloned.1.call-done, bf16[240,8640]{1,0:T(8,128)(2,1)} %dynamic-slice_bitcast_fusion), kind=kOutput, calls=%fused_computation.17 | convolution fusion | flops 707788800 | bytes 4919296 | tf_op jit(solution)/shard_map/dot_general | solution.py:138
  76.6 0.0 copy-done
  76.6 3.2 %fusion.10 = f32[512,240]{0,1:T(8,128)} fusion(bf16[512,2880]{1,0:T(8,128)(2,1)S(1)} %copy-done, bf16[240,8640]{1,0:T(8,128)(2,1)} %dynamic-slice_bitcast_fusion), kind=kOutput, calls=%fused_computation.16 | convolution fusion | flops 707788800 | bytes 4853760 | tf_op jit(solution)/shard_map/dot_general | solution.py:139
  79.8 62.5 %all-gather.3.cloned.1.call-done = f32[512,2885]{1,0:T(8,128)} async-done(((f32[16,2885]{1,0:T(8,128)}), f32[512,2885]{1,0:T(8,128)}) %all-gather.3.cloned.1.call-update) | async-done | bytes 5908496 | tf_op jit(solution)/shard_map/all_gather | solution.py:122
  142.3 1.2 fusion.17
  143.5 0.0 copy-start.1
  143.5 4.7 %select_convert_fusion.1 = (bf16[512,240]{0,1:T(8,128)(2,1)S(1)}, bf16[512,240]{0,1:T(8,128)(2,1)S(1)}) fusion(pred[240]{0:T(512)(128)(4,1)S(1)} %add_compare_fusion, f32[512,240]{0,1:T(8,128)} %fusion.13, f32[512,240]{0,1:T(8,128)} %fusion.10, bf16[240,8640]{1,0:T(8,128)(2,1)} %dynamic-slice_bitcast_fusion, f32[512,2885]{1,0:T(8,128)} %all-gather.3.cloned.1.call-done, ...), kind=kOutput, calls=%fused_computation.19 | convolution fusion | flops 712581120 | bytes 8919280 | tf_op jit(solution)/shard_map/dot_general | solution.py:140
  148.2 1.0 fusion.3
  149.2 3.8 %convolution_add_fusion = f32[512,2880]{1,0:T(8,128)} fusion(f32[512,2880]{1,0:T(8,128)S(1)} %fusion.3, bf16[512,240]{0,1:T(8,128)(2,1)S(1)} %get-tuple-element.2, bf16[240,8640]{1,0:T(8,128)(2,1)S(1)} %copy-done.1), kind=kOutput, calls=%fused_computation.2 | convolution fusion | flops 709263360 | bytes 13586432 | tf_op jit(solution)/shard_map/dot_general | solution.py:147
  153.0 0.0 reduce-scatter.2.cloned.1.call-update
  153.0 2.1 convolution_convert_fusion.1
  155.1 2.0 convolution_convert_fusion.2
  157.1 5.1 %convolution_convert_fusion = bf16[240,2880]{1,0:T(8,128)(2,1)} fusion(f32[512,240]{0,1:T(8,128)S(1)} %copy-done.5, pred[240]{0:T(512)(128)(4,1)S(1)} %add_compare_fusion, f32[512,240]{0,1:T(8,128)S(1)} %copy-done.4, f32[512,2885]{1,0:T(8,128)} %all-gather.3.cloned.1.call-done, f32[512]{0:T(512)S(1)} %fusion.17), kind=kOutput, calls=%fused_computation.4 | convolution fusion | flops 712289280 | bytes 8276208 | tf_op jit(solution)/shard_map/dot_general | solution.py:153
  162.2 0.0 copy-done.3
  162.2 7.5 %concatenate.7 = bf16[240,8640]{1,0:T(8,128)(2,1)} concatenate(bf16[240,2880]{1,0:T(8,128)(2,1)S(1)} %copy-done.3, bf16[240,2880]{1,0:T(8,128)(2,1)S(1)} %copy-done.2, bf16[240,2880]{1,0:T(8,128)(2,1)} %convolution_convert_fusion), dimensions={1} | concatenate | bytes 8294400 | tf_op jit(solution)/shard_map/concatenate | solution.py:151
  169.7 127.7 %reduce-scatter.2.cloned.1.call-done = f32[16,2880]{1,0:T(8,128)} async-done(((f32[512,2880]{1,0:T(8,128)}), f32[16,2880]{1,0:T(8,128)}) %reduce-scatter.2.cloned.1.call-update) | async-done | bytes 184336 | tf_op jit(solution)/shard_map/reduce_scatter | solution.py:150
  297.5 1.6 convert_element_type.31
  (9 shorter events, 0.0 us)
Async XLA Ops:
  7.2 65.2 %all-gather.5.cloned.1.call-start = ((), (), s32[]{:S(2)}) async-start(), calls=%async_computation.2 | async-start | bytes 3108864 | tf_op jit(solution)/shard_map/all_gather | solution.py:120
  7.9 134.4 %all-gather.3.cloned.1.call-start = ((), (), s32[]{:S(2)}) async-start(), calls=%async_computation.1 | async-start | bytes 6217728 | tf_op jit(solution)/shard_map/all_gather | solution.py:122
  10.4 287.0 %reduce-scatter.2.cloned.1.call-start = ((), (), s32[]{:S(2)}) async-start(), calls=%async_computation.3 | async-start | bytes 6217728 | tf_op jit(solution)/shard_map/reduce_scatter | solution.py:150
  72.4 4.2 %copy-start = (bf16[512,2880]{1,0:T(8,128)(2,1)S(1)}, bf16[512,2880]{1,0:T(8,128)(2,1)}, u32[]{:S(2)}) copy-start(bf16[512,2880]{1,0:T(8,128)(2,1)} %all-gather.5.cloned.1.call-done) | copy-start | bytes 8847364
  143.5 4.7 %copy-start.1 = (bf16[240,8640]{1,0:T(8,128)(2,1)S(1)}, bf16[240,8640]{1,0:T(8,128)(2,1)}, u32[]{:S(2)}) copy-start(bf16[240,8640]{1,0:T(8,128)(2,1)} %dynamic-slice_bitcast_fusion) | copy-start | bytes 12441604
  155.1 2.0 copy-start.4
  155.1 2.0 copy-start.5
  157.1 5.1 %copy-start.2 = (bf16[240,2880]{1,0:T(8,128)(2,1)S(1)}, bf16[240,2880]{1,0:T(8,128)(2,1)}, u32[]{:S(2)}) copy-start(bf16[240,2880]{1,0:T(8,128)(2,1)} %convolution_convert_fusion.1) | copy-start | bytes 4147204
  157.1 5.1 %copy-start.3 = (bf16[240,2880]{1,0:T(8,128)(2,1)S(1)}, bf16[240,2880]{1,0:T(8,128)(2,1)}, u32[]{:S(2)}) copy-start(bf16[240,2880]{1,0:T(8,128)(2,1)} %convolution_convert_fusion.2) | copy-start | bytes 4147204
Sparse Core Ops, SparseCore 0:
  10.8 61.5 all-gather.4
  75.2 66.9 all-gather.2
  153.1 144.2 reduce-scatter.1
